TPU v7x, 32 devices: a whole 2x2x4 slice. The times are simulated.
32 devices in a mesh: wide: 8 (over y, x, core), narrow: 4 (over z).
Axes of the slice: x: 2, y: 2, z: 4, core: 2. Of those that a mesh axis runs over, the one named last changes fastest.
Arguments:
- tokens: bfloat16 [32, 1536, 768], P(('wide', 'narrow')), may hold values from -6 to 6
- lengths: int32 [8, 4], P('wide'), may hold values from 1 to 1536, 4608 in all within a row
- qkv_weight: bfloat16 [768, 3, 768], P(None, None, 'narrow'), may hold values from -0.3125 to 0.3125
- qkv_bias: bfloat16 [3, 768], P(None, 'narrow'), may hold values from -3 to 3
- out_weight: bfloat16 [768, 768], P('narrow'), may hold values from -2.5 to 2.5
- out_bias: bfloat16 [768], replicated, may hold values from -2 to 2
- norm1_gain: bfloat16 [768], replicated, may hold values from 0.099609375 to 1.8984375
- norm1_shift: bfloat16 [768], replicated, may hold values from -2 to 2
- up_weight: bfloat16 [768, 3072], P(None, 'narrow'), may hold values from -0.21875 to 0.21875
- up_bias: bfloat16 [3072], P('narrow'), may hold values from -2 to 2
- down_weight: bfloat16 [3072, 768], P('narrow'), may hold values from -0.109375 to 0.109375
- down_bias: bfloat16 [768], replicated, may hold values from -2 to 2
- norm2_gain: bfloat16 [768], replicated, may hold values from 0.099609375 to 1.8984375
- norm2_shift: bfloat16 [768], replicated, may hold values from -2 to 2
- cotangent: bfloat16 [32, 1536, 768], P(('wide', 'narrow')), may hold values from -6 to 6
Outputs:
- output: bfloat16 [32, 1536, 768], P(('wide', 'narrow'))
- input_grad: float32 [32, 1536, 768], P(('wide', 'narrow'))
- grad_qkv_weight: float32 [768, 3, 768], P(None, None, 'narrow')
- grad_qkv_bias: float32 [3, 768], P(None, 'narrow')
- grad_out_weight: float32 [768, 768], P('narrow')
- grad_out_bias: float32 [768], replicated
- grad_norm1_gain: float32 [768], replicated
- grad_norm1_shift: float32 [768], replicated
- grad_up_weight: float32 [768, 3072], P(None, 'narrow')
- grad_up_bias: float32 [3072], P('narrow')
- grad_down_weight: float32 [3072, 768], P('narrow')
- grad_down_bias: float32 [768], replicated
- grad_norm2_gain: float32 [768], replicated
- grad_norm2_shift: float32 [768], replicated
Inputs may be any that keep to these rules, and one draw needn't show every extreme that they name: The 4 lengths of each wide index sum to 4608; positions at or beyond a slot's length are keys that no query attends to.
All inputs are finite; a program needn't handle non-finite values.
Results may differ from a plain program's by a relative error of at most 0.018.
The roundings to bfloat16 on the way count: a program that leaves them out, or rounds other values in their place, can miss the bound.
Values may be sent and summed in bfloat16 or wider, within the bound.
No kernel may reach another device: no remote copies, remote signals or barrier semaphores. Data moves between devices by JAX's collectives and lax.ppermute only.
A program may use at most 256 MiB of HBM per device.

v0:
```python
import jax
import jax.numpy as jnp
from jax import lax
from jax.sharding import PartitionSpec as P

HEADS = 12
HD = 64
NORM_EPS = 1e-06
MASK_VALUE = -1000000000.0


def rotary_tables(capacity, head_dim):
    positions = jnp.arange(capacity).astype(jnp.float32)
    frequencies = 10000.0 ** (-2.0 * jnp.arange(head_dim // 2).astype(jnp.float32) / head_dim)
    angles = positions[:, None] * frequencies[None, :]
    return (jnp.cos(angles)[:, None, :], jnp.sin(angles)[:, None, :])


def rotate(values, cosine, sine):
    half_dim = values.shape[-1] // 2
    first_half = values[..., :half_dim]
    second_half = values[..., half_dim:]
    return jnp.concatenate(
        [first_half * cosine - second_half * sine, second_half * cosine + first_half * sine],
        axis=-1,
    )


def norm_forward(values, gain_vec, shift_vec):
    row_mean = jnp.mean(values, axis=-1, keepdims=True)
    centred = values - row_mean
    inv_std = lax.rsqrt(jnp.mean(centred * centred, axis=-1, keepdims=True) + NORM_EPS)
    normed = centred * inv_std
    return (normed * gain_vec + shift_vec, normed, inv_std)


def norm_backward(upstream, normed, inv_std, gain_vec):
    scaled = upstream * gain_vec
    inner = (
        scaled
        - jnp.mean(scaled, axis=-1, keepdims=True)
        - normed * jnp.mean(scaled * normed, axis=-1, keepdims=True)
    )
    gain_grad = jnp.sum(upstream * normed, axis=(0, 1))
    shift_grad = jnp.sum(upstream, axis=(0, 1))
    return (inv_std * inner, gain_grad, shift_grad)


def to_items(values, group_count):
    slot_count, capacity, head_count, head_dim = values.shape
    values = values.reshape(slot_count, capacity, group_count, head_count // group_count, head_dim)
    values = values.transpose(0, 2, 1, 3, 4)
    return values.reshape(slot_count * group_count, capacity, head_count // group_count, head_dim)


def from_items(values, group_count):
    item_count, capacity, group_heads, head_dim = values.shape
    values = values.reshape(item_count // group_count, group_count, capacity, group_heads, head_dim)
    values = values.transpose(0, 2, 1, 3, 4)
    return values.reshape(item_count // group_count, capacity, group_count * group_heads, head_dim)


def attend_forward(query_item, key_item, value_item, item_length, block_rows, score_scale):
    capacity = query_item.shape[0]
    live_keys = jnp.arange(capacity) < item_length

    def one_block(offset):
        query_block = lax.dynamic_slice_in_dim(query_item, offset, block_rows, 0)
        scores = (
            jnp.einsum("qhe,khe->hqk", query_block, key_item, preferred_element_type=jnp.float32)
            * score_scale
        )
        scores = jnp.where(live_keys[None, None, :], scores, MASK_VALUE)
        row_max = jnp.max(scores, axis=-1, keepdims=True)
        exponentials = jnp.exp(scores - row_max)
        denominator = jnp.sum(exponentials, axis=-1, keepdims=True)
        weights = (exponentials / denominator).astype(jnp.bfloat16)
        context = jnp.einsum(
            "hqk,khe->qhe", weights, value_item, preferred_element_type=jnp.float32
        )
        return (context, (row_max + jnp.log(denominator))[..., 0])

    offsets = jnp.arange(capacity // block_rows) * block_rows
    context, log_sums = lax.map(one_block, offsets)
    return (context.reshape(query_item.shape), log_sums)


def attend_backward(
    query_item, key_item, value_item, grad_item, log_sums, item_length, block_rows, score_scale
):
    capacity = query_item.shape[0]
    live_keys = jnp.arange(capacity) < item_length

    def one_block(carry, inputs):
        key_grad, value_grad = carry
        offset, block_sums = inputs
        query_block = lax.dynamic_slice_in_dim(query_item, offset, block_rows, 0)
        grad_block = lax.dynamic_slice_in_dim(grad_item, offset, block_rows, 0)
        scores = (
            jnp.einsum("qhe,khe->hqk", query_block, key_item, preferred_element_type=jnp.float32)
            * score_scale
        )
        scores = jnp.where(live_keys[None, None, :], scores, MASK_VALUE)
        weights = jnp.exp(scores - block_sums[..., None])
        weight_grad = jnp.einsum(
            "qhe,khe->hqk", grad_block, value_item, preferred_element_type=jnp.float32
        )
        row_dot = jnp.sum(weight_grad * weights, axis=-1, keepdims=True)
        score_grad = (weights * (weight_grad - row_dot)).astype(jnp.bfloat16)
        query_grad = (
            jnp.einsum("hqk,khe->qhe", score_grad, key_item, preferred_element_type=jnp.float32)
            * score_scale
        )
        key_grad = (
            key_grad
            + jnp.einsum(
                "hqk,qhe->khe", score_grad, query_block, preferred_element_type=jnp.float32
            )
            * score_scale
        )
        value_grad = value_grad + jnp.einsum(
            "hqk,qhe->khe",
            weights.astype(jnp.bfloat16),
            grad_block,
            preferred_element_type=jnp.float32,
        )
        return ((key_grad, value_grad), query_grad)

    offsets = jnp.arange(capacity // block_rows) * block_rows
    zero_rows = jnp.zeros(key_item.shape, jnp.float32)
    (key_grad, value_grad), query_grad = lax.scan(
        one_block, (zero_rows, zero_rows), (offsets, log_sums)
    )
    return (query_grad.reshape(key_item.shape), key_grad, value_grad)


def shards(
    tokens,
    lengths,
    qkv_weight,
    qkv_bias,
    out_weight,
    out_bias,
    norm1_gain,
    norm1_shift,
    up_weight,
    up_bias,
    down_weight,
    down_bias,
    norm2_gain,
    norm2_shift,
    cotangent,
):
    narrow_size = lax.axis_size("narrow")
    slot_dev, capacity, features = tokens.shape
    group_heads = HEADS // narrow_size
    score_scale = HD ** (-0.5)
    block_rows = min(capacity, 512)
    cosine, sine = rotary_tables(capacity, HD)
    all_lengths = lengths.reshape(-1)
    gain_one = norm1_gain.astype(jnp.float32)
    shift_one = norm1_shift.astype(jnp.float32)
    gain_two = norm2_gain.astype(jnp.float32)
    shift_two = norm2_shift.astype(jnp.float32)
    qkv_local, qkv_bias_local, out_local = (qkv_weight, qkv_bias, out_weight)
    up_local, up_bias_local, down_local = (up_weight, up_bias, down_weight)
    row_tokens = lax.all_gather(tokens, "narrow", axis=0, tiled=True)
    slot_count = row_tokens.shape[0]
    projected = jnp.einsum(
        "scd,dje->scje", row_tokens, qkv_local, preferred_element_type=jnp.float32
    ) + qkv_bias_local.astype(jnp.float32)
    head_count = projected.shape[3] // HD
    group_count = head_count // group_heads
    head_shape = (slot_count, capacity, head_count, HD)
    queries = rotate(projected[:, :, 0].reshape(head_shape), cosine, sine).astype(jnp.bfloat16)
    key_rows = rotate(projected[:, :, 1].reshape(head_shape), cosine, sine).astype(jnp.bfloat16)
    value_rows = projected[:, :, 2].reshape(head_shape).astype(jnp.bfloat16)
    item_lengths = jnp.repeat(all_lengths, group_count)
    query_items = to_items(queries, group_count)
    key_items = to_items(key_rows, group_count)
    value_items = to_items(value_rows, group_count)

    def forward_item(item):
        return attend_forward(item[0], item[1], item[2], item[3], block_rows, score_scale)

    context_items, log_sums = lax.map(
        forward_item, (query_items, key_items, value_items, item_lengths)
    )
    context = (
        from_items(context_items, group_count)
        .reshape(slot_count, capacity, head_count * HD)
        .astype(jnp.bfloat16)
    )
    attn_terms = jnp.einsum("scd,de->sce", context, out_local, preferred_element_type=jnp.float32)
    attended = lax.psum_scatter(attn_terms, "narrow", scatter_dimension=0, tiled=True)
    own_tokens = tokens.astype(jnp.float32)
    hidden, normed_one, inv_one = norm_forward(
        own_tokens + attended + out_bias.astype(jnp.float32), gain_one, shift_one
    )
    hidden_low = hidden.astype(jnp.bfloat16)
    hidden_rows = lax.all_gather(hidden_low, "narrow", axis=0, tiled=True)
    upward = jnp.einsum(
        "scd,df->scf", hidden_rows, up_local, preferred_element_type=jnp.float32
    ) + up_bias_local.astype(jnp.float32)
    active = jax.nn.gelu(upward, approximate=False).astype(jnp.bfloat16)
    down_terms = jnp.einsum("scf,fd->scd", active, down_local, preferred_element_type=jnp.float32)
    downward = lax.psum_scatter(down_terms, "narrow", scatter_dimension=0, tiled=True)
    output_value, normed_two, inv_two = norm_forward(
        hidden + downward + down_bias.astype(jnp.float32), gain_two, shift_two
    )
    output = output_value.astype(jnp.bfloat16)
    pre_two_grad, gain_two_grad, shift_two_grad = norm_backward(
        cotangent.astype(jnp.float32), normed_two, inv_two, gain_two
    )
    down_bias_grad = jnp.sum(pre_two_grad, axis=(0, 1))
    pre_two_low = pre_two_grad.astype(jnp.bfloat16)
    down_grad_rows = lax.all_gather(pre_two_low, "narrow", axis=0, tiled=True)
    down_grad = jnp.einsum(
        "scf,scd->fd", active, down_grad_rows, preferred_element_type=jnp.float32
    )
    active_grad = jnp.einsum(
        "scd,fd->scf", down_grad_rows, down_local, preferred_element_type=jnp.float32
    )
    ignored_value, gelu_pull = jax.vjp(lambda inner: jax.nn.gelu(inner, approximate=False), upward)
    upward_grad = gelu_pull(active_grad)[0]
    up_bias_grad = jnp.sum(upward_grad, axis=(0, 1))
    upward_low = upward_grad.astype(jnp.bfloat16)
    up_grad = jnp.einsum("scd,scf->df", hidden_rows, upward_low, preferred_element_type=jnp.float32)
    hidden_terms = jnp.einsum(
        "scf,df->scd", upward_low, up_local, preferred_element_type=jnp.float32
    )
    hidden_grad = lax.psum_scatter(hidden_terms, "narrow", scatter_dimension=0, tiled=True)
    pre_one_grad, gain_one_grad, shift_one_grad = norm_backward(
        hidden_grad + pre_two_grad, normed_one, inv_one, gain_one
    )
    out_bias_grad = jnp.sum(pre_one_grad, axis=(0, 1))
    pre_one_low = pre_one_grad.astype(jnp.bfloat16)
    out_grad_rows = lax.all_gather(pre_one_low, "narrow", axis=0, tiled=True)
    out_grad = jnp.einsum("scd,sce->de", context, out_grad_rows, preferred_element_type=jnp.float32)
    context_grad = jnp.einsum(
        "sce,de->scd", out_grad_rows, out_local, preferred_element_type=jnp.float32
    ).astype(jnp.bfloat16)
    grad_items = to_items(context_grad.reshape(head_shape), group_count)

    def backward_item(item):
        return attend_backward(
            item[0], item[1], item[2], item[3], item[4], item[5], block_rows, score_scale
        )

    query_grad, key_grad, value_grad = lax.map(
        backward_item, (query_items, key_items, value_items, grad_items, log_sums, item_lengths)
    )
    flat_shape = (slot_count, capacity, head_count * HD)
    query_grad = rotate(from_items(query_grad, group_count), cosine, -sine).reshape(flat_shape)
    key_grad = rotate(from_items(key_grad, group_count), cosine, -sine).reshape(flat_shape)
    value_grad = from_items(value_grad, group_count).reshape(flat_shape)
    projected_grad = jnp.stack([query_grad, key_grad, value_grad], axis=2)
    qkv_bias_grad = jnp.sum(projected_grad, axis=(0, 1))
    projected_low = projected_grad.astype(jnp.bfloat16)
    qkv_grad = jnp.einsum(
        "scd,scje->dje", row_tokens, projected_low, preferred_element_type=jnp.float32
    )
    input_terms = jnp.einsum(
        "scje,dje->scd", projected_low, qkv_local, preferred_element_type=jnp.float32
    )
    input_part = lax.psum_scatter(
        input_terms.astype(jnp.bfloat16), "narrow", scatter_dimension=0, tiled=True
    ).astype(jnp.float32)
    input_grad = input_part + pre_one_grad
    small_grads = lax.psum(
        (
            gain_one_grad,
            shift_one_grad,
            gain_two_grad,
            shift_two_grad,
            out_bias_grad,
            down_bias_grad,
        ),
        "narrow",
    )
    summed = lax.psum(
        (
            qkv_grad,
            qkv_bias_grad,
            out_grad,
            small_grads[4],
            small_grads[0],
            small_grads[1],
            up_grad,
            up_bias_grad,
            down_grad,
            small_grads[5],
            small_grads[2],
            small_grads[3],
        ),
        "wide",
    )
    return (
        output,
        input_grad,
        summed[0],
        summed[1],
        summed[2],
        summed[3],
        summed[4],
        summed[5],
        summed[6],
        summed[7],
        summed[8],
        summed[9],
        summed[10],
        summed[11],
    )


def solution(mesh):
    placed = (
        P(("wide", "narrow"), None, None),
        P("wide", None),
        P(None, None, "narrow"),
        P(None, "narrow"),
        P("narrow", None),
        P(),
        P(),
        P(),
        P(None, "narrow"),
        P("narrow"),
        P("narrow", None),
        P(),
        P(),
        P(),
        P(("wide", "narrow"), None, None),
    )
    return jax.shard_map(
        shards,
        mesh=mesh,
        in_specs=placed,
        out_specs=(
            P(("wide", "narrow"), None, None),
            P(("wide", "narrow"), None, None),
            P(None, None, "narrow"),
            P(None, "narrow"),
            P("narrow", None),
            P(),
            P(),
            P(),
            P(None, "narrow"),
            P("narrow"),
            P("narrow", None),
            P(),
            P(),
            P(),
        ),
        check_vma=False,
    )
```

profile of v0, /device:TPU:0, one launch (start us, length us, event | category | flops | bytes accessed | tf_op | source)
XLA Modules:
  0.0 2778.9 jit_solution(16459754968414012674)
XLA Ops:
  11.8 167.4 %all-gather.5.cloned.1.call-done = bf16[4,1536,768]{2,1,0:T(8,128)(2,1)} async-done(((bf16[1,1536,768]{2,1,0:T(8,128)(2,1)}), bf16[4,1536,768]{2,1,0:T(8,128)(2,1)}) %all-gather.5.cloned.1.call-update) | async-done | bytes 9437200 | tf_op jit(solution)/shard_map/all_gather | solution.py:167
  179.1 12.4 fusion.47
  204.4 152.3 %while.61 = (s32[]{:T(128)}, bf16[4,1536,3,64]{1,3,2,0:T(8,128)(2,1)}, f32[4,3,3,512]{3,2,1,0:T(4,128)}, bf16[4,1536,3,64]{1,3,2,0:T(8,128)(2,1)}, bf16[4,1536,3...) while((s32[]{:T(128)}, ...), condition=%wide.region_5.6_spmd.clone, body=%wide.region_0.5_spmd.sunk.clone | while | flops 632291328 | bytes 37272460 | solution.py:186
  207.4 30.9 %while.60 = (s32[]{:T(128)}, bf16[3,512,3,64]{1,3,2,0:T(8,128)(2,1)S(1)}, f32[3,3,512]{2,1,0:T(4,128)}, s32[3]{0:T(128)S(1)}, bf16[1536,3,64]{0,2,1:T(8,128)(2,1...) while((s32[]{:T(128)}, ...), condition=%wide.region_4.4_spmd.clone, body=%wide.region_1.3_spmd.clone.sunk | while | flops 632291328 | bytes 30144168 | solution.py:84
  245.5 30.9 %while.60 = (s32[]{:T(128)}, bf16[3,512,3,64]{1,3,2,0:T(8,128)(2,1)S(1)}, f32[3,3,512]{2,1,0:T(4,128)}, s32[3]{0:T(128)S(1)}, bf16[1536,3,64]{0,2,1:T(8,128)(2,1...) while((s32[]{:T(128)}, ...), condition=%wide.region_4.4_spmd.clone, body=%wide.region_1.3_spmd.clone.sunk | while | flops 632291328 | bytes 30144168 | solution.py:84
  283.5 30.9 %while.60 = (s32[]{:T(128)}, bf16[3,512,3,64]{1,3,2,0:T(8,128)(2,1)S(1)}, f32[3,3,512]{2,1,0:T(4,128)}, s32[3]{0:T(128)S(1)}, bf16[1536,3,64]{0,2,1:T(8,128)(2,1...) while((s32[]{:T(128)}, ...), condition=%wide.region_4.4_spmd.clone, body=%wide.region_1.3_spmd.clone.sunk | while | flops 632291328 | bytes 30144168 | solution.py:84
  321.6 30.9 %while.60 = (s32[]{:T(128)}, bf16[3,512,3,64]{1,3,2,0:T(8,128)(2,1)S(1)}, f32[3,3,512]{2,1,0:T(4,128)}, s32[3]{0:T(128)S(1)}, bf16[1536,3,64]{0,2,1:T(8,128)(2,1...) while((s32[]{:T(128)}, ...), condition=%wide.region_4.4_spmd.clone, body=%wide.region_1.3_spmd.clone.sunk | while | flops 632291328 | bytes 30144168 | solution.py:84
  356.7 10.8 fusion.79
  368.2 311.4 %reduce-scatter.5.cloned.1.call-done = f32[1,1536,768]{2,1,0:T(8,128)} async-done(((f32[4,1536,768]{2,1,0:T(8,128)}), f32[1,1536,768]{2,1,0:T(8,128)}) %reduce-scatter.5.cloned.1.call-update) | async-done | bytes 4718608 | tf_op jit(solution)/shard_map/reduce_scatter | solution.py:195
  687.0 167.9 %all-gather.7.cloned.1.call-done = bf16[4,1536,768]{2,1,0:T(8,128)(2,1)} async-done(((bf16[1,1536,768]{2,1,0:T(8,128)(2,1)}), bf16[4,1536,768]{2,1,0:T(8,128)(2,1)}) %all-gather.7.cloned.1.call-update) | async-done | bytes 9437200 | tf_op jit(solution)/shard_map/all_gather | solution.py:201
  855.0 19.3 fusion.62
  874.3 46.0 %multiply_convert_fusion.1 = (bf16[4,1536,768]{2,1,0:T(8,128)(2,1)S(1)}, f32[4,1536,768]{2,1,0:T(8,128)}) fusion(f32[4,1536,768]{2,1,0:T(8,128)} %get-tuple-element.438, f32[768]{0:T(1024)S(1)} %convert_element_type.166, u8[1536,768]{1,0:T(8,128)(4,1)S(1)} %get-tuple-element.302, u8[1536,768]{1,0:T(8,128)(4,1)S(1)} %get-tuple-element.301), kind=kLoop, calls=%fused_computation.65 | loop fusion | flops 335020032 | bytes 49548288 | tf_op jit(solution)/shard_map/convert_element_type | solution.py:205
  924.0 10.5 fusion.71
  935.2 311.4 %reduce-scatter.7.cloned.1.call-done = f32[1,1536,768]{2,1,0:T(8,128)} async-done(((f32[4,1536,768]{2,1,0:T(8,128)}), f32[1,1536,768]{2,1,0:T(8,128)}) %reduce-scatter.7.cloned.1.call-update) | async-done | bytes 4718608 | tf_op jit(solution)/shard_map/reduce_scatter | solution.py:207
  1263.6 168.0 %all-gather.9.cloned.1.call-done = bf16[4,1536,768]{2,1,0:T(8,128)(2,1)} async-done(((bf16[1,1536,768]{2,1,0:T(8,128)(2,1)}), bf16[4,1536,768]{2,1,0:T(8,128)(2,1)}) %all-gather.9.cloned.1.call-update) | async-done | bytes 9437200 | tf_op jit(solution)/shard_map/all_gather | solution.py:217
  1431.6 25.3 fusion.91
  1456.8 14.4 fusion.59
  1471.3 312.1 %reduce-scatter.9.cloned.1.call-done = f32[1,1536,768]{2,1,0:T(8,128)} async-done(((f32[4,1536,768]{2,1,0:T(8,128)}), f32[1,1536,768]{2,1,0:T(8,128)}) %reduce-scatter.9.cloned.1.call-update) | async-done | bytes 4718608 | tf_op jit(solution)/shard_map/reduce_scatter | solution.py:232
  1783.4 7.0 multiply_reduce_fusion.1
  1798.7 168.0 %all-gather.11.cloned.1.call-done = bf16[4,1536,768]{2,1,0:T(8,128)(2,1)} async-done(((bf16[1,1536,768]{2,1,0:T(8,128)(2,1)}), bf16[4,1536,768]{2,1,0:T(8,128)(2,1)}) %all-gather.11.cloned.1.call-update) | async-done | bytes 9437200 | tf_op jit(solution)/shard_map/all_gather | solution.py:238
  1966.7 6.9 convolution_convert_fusion
  1979.2 481.4 %while.63 = (s32[]{:T(128)}, f32[4,1536,3,64]{1,3,2,0:T(8,128)}, f32[4,1536,3,64]{1,3,2,0:T(8,128)}, f32[4,1536,3,64]{1,3,2,0:T(8,128)}, f32[4,3,3,512]{3,2,1,0:...) while((s32[]{:T(128)}, f32[4,1536,3,64]{1,3,2,0:T(8,128)}, ...), condition=%wide.region_21.22_spmd.clone, body=%wide.region_17.21_spmd.sunk.clone | while | flops 1532755968 | bytes 175250576 | solution.py:250
  1986.7 104.4 %while.62 = (s32[]{:T(128)}, f32[1536,3,64]{0,2,1:T(8,128)S(1)}, f32[1536,3,64]{0,2,1:T(8,128)S(1)}, f32[3,512,3,64]{1,3,2,0:T(8,128)}, s32[3]{0:T(128)S(1)}, /*...) while((s32[]{:T(128)}, f32[1536,3,64]{0,2,1:T(8,128)S(1)}, ...), condition=%wide.region_20.20_spmd.clone, body=%wide.region_18.19_spmd.clone.sunk | while | flops 1532755968 | bytes 135104288 | solution.py:131
  1994.4 6.6 multiply_reduce_fusion.7
  2001.0 9.4 multiply_convert_fusion.3
  2016.6 5.0 fusion.138
  2029.3 6.6 multiply_reduce_fusion.7
  2035.8 9.4 multiply_convert_fusion.3
  2051.4 5.0 fusion.138
  2064.1 6.5 multiply_reduce_fusion.7
  2070.6 9.4 multiply_convert_fusion.3
  2107.1 104.4 %while.62 = (s32[]{:T(128)}, f32[1536,3,64]{0,2,1:T(8,128)S(1)}, f32[1536,3,64]{0,2,1:T(8,128)S(1)}, f32[3,512,3,64]{1,3,2,0:T(8,128)}, s32[3]{0:T(128)S(1)}, /*...) while((s32[]{:T(128)}, f32[1536,3,64]{0,2,1:T(8,128)S(1)}, ...), condition=%wide.region_20.20_spmd.clone, body=%wide.region_18.19_spmd.clone.sunk | while | flops 1532755968 | bytes 135104288 | solution.py:131
  2114.8 6.6 multiply_reduce_fusion.7
  2121.3 9.4 multiply_convert_fusion.3
  2149.6 6.6 multiply_reduce_fusion.7
  2156.2 9.4 multiply_convert_fusion.3
  2184.4 6.5 multiply_reduce_fusion.7
  2190.9 9.4 multiply_convert_fusion.3
  2227.3 104.4 %while.62 = (s32[]{:T(128)}, f32[1536,3,64]{0,2,1:T(8,128)S(1)}, f32[1536,3,64]{0,2,1:T(8,128)S(1)}, f32[3,512,3,64]{1,3,2,0:T(8,128)}, s32[3]{0:T(128)S(1)}, /*...) while((s32[]{:T(128)}, f32[1536,3,64]{0,2,1:T(8,128)S(1)}, ...), condition=%wide.region_20.20_spmd.clone, body=%wide.region_18.19_spmd.clone.sunk | while | flops 1532755968 | bytes 135104288 | solution.py:131
  2235.0 6.6 multiply_reduce_fusion.7
  2241.6 9.4 multiply_convert_fusion.3
  2269.9 6.6 multiply_reduce_fusion.7
  2276.4 9.4 multiply_convert_fusion.3
  2304.7 6.5 multiply_reduce_fusion.7
  2311.2 9.4 multiply_convert_fusion.3
  2347.6 104.4 %while.62 = (s32[]{:T(128)}, f32[1536,3,64]{0,2,1:T(8,128)S(1)}, f32[1536,3,64]{0,2,1:T(8,128)S(1)}, f32[3,512,3,64]{1,3,2,0:T(8,128)}, s32[3]{0:T(128)S(1)}, /*...) while((s32[]{:T(128)}, f32[1536,3,64]{0,2,1:T(8,128)S(1)}, ...), condition=%wide.region_20.20_spmd.clone, body=%wide.region_18.19_spmd.clone.sunk | while | flops 1532755968 | bytes 135104288 | solution.py:131
  2355.3 6.6 multiply_reduce_fusion.7
  2361.9 9.4 multiply_convert_fusion.3
  2390.1 6.6 multiply_reduce_fusion.7
  2396.7 9.4 multiply_convert_fusion.3
  2425.0 6.5 multiply_reduce_fusion.7
  2431.5 9.4 multiply_convert_fusion.3
  2460.6 6.5 multiply_subtract_fusion.1
  2473.7 10.2 bitcast_convert_fusion
  2484.0 15.1 convolution_bitcast_fusion
  2499.2 14.0 fusion.64
  2513.2 6.5 convolution_bitcast_fusion.1
  2519.8 6.8 fusion.67
  2527.4 19.0 all-reduce.2
  2546.4 5.9 fusion.41
  2552.4 23.8 all-reduce
  2576.2 68.3 %reduce-scatter.11.cloned.1.call-done = bf16[1,1536,768]{2,1,0:T(8,128)(2,1)} async-done(((bf16[4,1536,768]{2,1,0:T(8,128)(2,1)}), bf16[1,1536,768]{2,1,0:T(8,128)(2,1)}) %reduce-scatter.11.cloned.1.call-update) | async-done | bytes 2359312 | tf_op jit(solution)/shard_map/reduce_scatter | solution.py:266
  2644.6 5.7 convert_add_fusion
  2650.3 113.9 %all-reduce.5.cloned.1.call-done = (f32[768,3,192]{0,2,1:T(8,128)}, f32[192,768]{1,0:T(8,128)}, f32[768,768]{1,0:T(8,128)}, f32[768,768]{1,0:T(8,128)}) async-done(((f32[768,3,192]{0,2,1:T(8,128)}, f32[192,768]{1,0:T(8,128)}, f32[768,768]{1,0:T(8,128)}, f32[768,768]{1,0:T(8,128)}), (f32[768,3,192]{0,2,1:T(8,128)}, f32[192,768]{1,0:T(8,128)}, f32[768,768]{1,0:T(8,128)}, ...) | async-done | bytes 7077904 | tf_op jit(solution)/shard_map/psum | solution.py:281
  (481 shorter events, 459.1 us)
Async XLA Ops:
  7.2 847.8 %copy-start = (bf16[768,768]{1,0:T(8,128)(2,1)S(1)}, bf16[768,768]{1,0:T(8,128)(2,1)}, u32[]{:S(2)}) copy-start(bf16[768,768]{1,0:T(8,128)(2,1)} %param.31) | copy-start | bytes 3538948
  7.2 171.9 %copy-start.36 = (bf16[768,3,192]{0,2,1:T(8,128)(2,1)S(1)}, bf16[768,3,192]{0,2,1:T(8,128)(2,1)}, u32[]{:S(2)}) copy-start(bf16[768,3,192]{0,2,1:T(8,128)(2,1)} %param.25) | copy-start | bytes 2654212
  7.2 171.9 %all-gather.5.cloned.1.call-start = ((), (), s32[]{:S(2)}) async-start(), calls=%async_computation.4 | async-start | bytes 11796480 | tf_op jit(solution)/shard_map/all_gather | solution.py:167
  7.9 671.7 %reduce-scatter.5.cloned.1.call-start = ((), (), s32[]{:S(2)}) async-start(), calls=%async_computation.5 | async-start | bytes 23592960 | tf_op jit(solution)/shard_map/reduce_scatter | solution.py:195
  11.8 188.6 %copy-start.19 = (f32[1536,32]{0,1:T(8,128)}, f32[1536,32]{0,1:T(8,128)S(1)}, u32[]{:S(2)}) copy-start(f32[1536,32]{0,1:T(8,128)S(1)} %get-tuple-element.437) | copy-start | bytes 589828
  367.5 312.2 %copy-start.13 = (bf16[1,1536,768]{2,1,0:T(8,128)(2,1)S(1)}, bf16[1,1536,768]{2,1,0:T(8,128)(2,1)}, u32[]{:S(2)}) copy-start(bf16[1,1536,768]{2,1,0:T(8,128)(2,1)} %param.23) | copy-start | bytes 7077892
  367.5 487.5 %all-gather.7.cloned.1.call-start = ((), (), s32[]{:S(2)}) async-start(), calls=%async_computation.6 | async-start | bytes 11796480 | tf_op jit(solution)/shard_map/all_gather | solution.py:201
  686.9 559.7 %reduce-scatter.7.cloned.1.call-start = ((), (), s32[]{:S(2)}) async-start(), calls=%async_computation.7 | async-start | bytes 23592960 | tf_op jit(solution)/shard_map/reduce_scatter | solution.py:207
  874.3 49.7 %copy-start.35 = (bf16[768,768]{1,0:T(8,128)(2,1)S(1)}, bf16[768,768]{1,0:T(8,128)(2,1)}, u32[]{:S(2)}) copy-start(bf16[768,768]{1,0:T(8,128)(2,1)} %param.33) | copy-start | bytes 3538948
  934.5 497.1 %all-gather.9.cloned.1.call-start = ((), (), s32[]{:S(2)}) async-start(), calls=%async_computation.8 | async-start | bytes 11796480 | tf_op jit(solution)/shard_map/all_gather | solution.py:217
  1263.6 519.8 %reduce-scatter.9.cloned.1.call-start = ((), (), s32[]{:S(2)}) async-start(), calls=%async_computation.9 | async-start | bytes 23592960 | tf_op jit(solution)/shard_map/reduce_scatter | solution.py:232
  1471.3 495.4 %all-gather.11.cloned.1.call-start = ((), (), s32[]{:S(2)}) async-start(), calls=%async_computation.10 | async-start | bytes 11796480 | tf_op jit(solution)/shard_map/all_gather | solution.py:238
  1797.0 169.7 %copy-start.20 = (bf16[192,768]{1,0:T(8,128)(2,1)S(1)}, bf16[192,768]{1,0:T(8,128)(2,1)}, u32[]{:S(2)}) copy-start(bf16[192,768]{1,0:T(8,128)(2,1)} %param.27) | copy-start | bytes 884740
  1798.7 845.9 %reduce-scatter.11.cloned.1.call-start = ((), (), s32[]{:S(2)}) async-start(), calls=%async_computation.11 | async-start | bytes 11796480 | tf_op jit(solution)/shard_map/reduce_scatter | solution.py:266
  1973.6 5.6 copy-start.39
  1979.4 7.4 copy-start.15
  1994.4 6.6 copy-start.2
  2010.4 3.9 copy-start.3
  2029.3 6.6 copy-start.2
  2045.2 3.9 copy-start.3
  2064.1 6.5 copy-start.2
  2080.0 3.8 copy-start.3
  2092.8 6.9 copy-start.16
  2099.7 7.3 copy-start.15
  2114.8 6.6 copy-start.2
  2130.7 3.9 copy-start.3
  2149.6 6.6 copy-start.2
  2165.6 3.9 copy-start.3
  2184.4 6.5 copy-start.2
  2200.3 3.8 copy-start.3
  2213.2 6.8 copy-start.16
  2220.0 7.3 copy-start.15
  2235.0 6.6 copy-start.2
  2251.0 3.9 copy-start.3
  2269.9 6.6 copy-start.2
  2285.8 3.9 copy-start.3
  2304.7 6.5 copy-start.2
  2320.6 3.8 copy-start.3
  2333.4 6.8 copy-start.16
  2340.3 7.3 copy-start.15
  2355.3 6.6 copy-start.2
  2371.3 3.9 copy-start.3
  2390.1 6.6 copy-start.2
  2406.1 3.9 copy-start.3
  2425.0 6.5 copy-start.2
  2440.9 3.8 copy-start.3
  2453.7 6.9 copy-start.16
  2467.1 6.3 slice-start.4
  2469.6 4.1 copy-start.37
  2483.9 280.3 %all-reduce.5.cloned.1.call-start = ((), (), s32[]{:S(2)}) async-start(), calls=%async_computation.12 | async-start | bytes 14155776 | tf_op jit(solution)/shard_map/psum | solution.py:281
  2484.0 35.7 %slice-start = ((s8[4718592]{0:T(1024)(128)(4,1)}), s8[4194304]{0:T(1024)(128)(4,1)S(1)}, s32[]{:S(2)}) async-start(s8[4718592]{0:T(1024)(128)(4,1)} %bitcast.204), calls=%async_computation.13 | async-start | bytes 8388608
  2484.0 35.7 %slice-start.2 = ((s8[4718592]{0:T(1024)(128)(4,1)}), s8[4194304]{0:T(1024)(128)(4,1)S(1)}, s32[]{:S(2)}) async-start(s8[4718592]{0:T(1024)(128)(4,1)} %bitcast.209), calls=%async_computation.15 | async-start | bytes 8388608
  2484.0 35.7 %slice-start.6 = ((s8[4718592]{0:T(1024)(128)(4,1)}), s8[4194304]{0:T(1024)(128)(4,1)S(1)}, s32[]{:S(2)}) async-start(s8[4718592]{0:T(1024)(128)(4,1)} %bitcast.216), calls=%async_computation.19 | async-start | bytes 8388608
  2484.0 35.7 %slice-start.8 = ((s8[9437184]{0:T(1024)(128)(4,1)}), s8[4194304]{0:T(1024)(128)(4,1)S(1)}, s32[]{:S(2)}) async-start(s8[9437184]{0:T(1024)(128)(4,1)} %bitcast.222), calls=%async_computation.21 | async-start | bytes 8388608
  2484.0 35.7 %slice-start.9 = ((s8[9437184]{0:T(1024)(128)(4,1)}), s8[4194304]{0:T(1024)(128)(4,1)S(1)}, s32[]{:S(2)}) async-start(s8[9437184]{0:T(1024)(128)(4,1)} %bitcast.222), calls=%async_computation.22 | async-start | bytes 8388608
  2499.1 14.1 copy-start.14
  2499.1 20.6 slice-start.1
  2499.1 20.6 slice-start.3
  2499.1 20.6 slice-start.7
  2499.2 20.6 slice-start.10
  2546.4 5.9 copy-start.27
  2764.2 5.0 copy-start.18
  2764.2 6.4 copy-start.17
  2767.2 4.8 copy-start.1
  (27 other events, 43.3 us)
Sparse Core Ops, SparseCore 0:
  9.6 169.4 all-gather.4
  367.6 311.9 reduce-scatter.4
  687.1 167.8 all-gather.6
  934.6 311.9 reduce-scatter.6
  1263.7 167.8 all-gather.8
  1471.4 311.9 reduce-scatter.8
  1798.8 167.8 all-gather.10
  2484.0 160.5 reduce-scatter.10
  2649.9 114.2 all-reduce.4
where the time goes:
time: 2790 us; the launch traced here: 2780 us
  waiting for transfers between devices  1790 us (64%)
  matrix products  459 us (16%)
  other arithmetic  266 us (10%)
  local copies, waits for them, and re-layouts  158 us (6%)
  loops' own time  49.1 us (2%)
  blocking collectives  42.9 us (2%)
    reduce_scatter x1, waiting for transfers between devices, shards(): lax.psum_scatter(hidden_terms, 'narrow', scatter_dimension=0, tiled=True)  312 us
    reduce_scatter x1, waiting for transfers between devices, shards(): lax.psum_scatter(attn_terms, 'narrow', scatter_dimension=0, tiled=True)  311 us
    reduce_scatter x1, waiting for transfers between devices, shards(): lax.psum_scatter(down_terms, 'narrow', scatter_dimension=0, tiled=True)  311 us
    all_gather x1, waiting for transfers between devices, shards(): down_grad_rows = lax.all_gather(pre_two_low, 'narrow', axis=0, tiled=True)  168 us
    all_gather x1, waiting for transfers between devices, shards(): out_grad_rows = lax.all_gather(pre_one_low, 'narrow', axis=0, tiled=True)  168 us
    all_gather x1, waiting for transfers between devices, shards(): hidden_rows = lax.all_gather(hidden_low, 'narrow', axis=0, tiled=True)  168 us
    all_gather x1, waiting for transfers between devices, shards(): row_tokens = lax.all_gather(tokens, 'narrow', axis=0, tiled=True)  167 us
    psum x1, waiting for transfers between devices, shards(): lax.psum((qkv_grad, qkv_bias_grad, out_grad, small_grads[4], small_grads[...  114 us
  transfers between devices with their start and end apart: 9, of which 9 were waited for; matrix products, arithmetic and copies ran while one was open for 2% of the time, Pallas kernels for 0%

commit v1 on v0

--- a/solution.py
+++ b/solution.py
@@ -7,6 +7,28 @@
 HD = 64
 NORM_EPS = 1e-06
 MASK_VALUE = -1000000000.0
+
+
+def joined_along(parts, dim):
+    parts = jnp.moveaxis(parts, 0, dim)
+    shape = parts.shape
+    return parts.reshape(*shape[:dim], shape[dim] * shape[dim + 1], *shape[dim + 2 :])
+
+
+def collected_by_bits(array, axis):
+    devices = lax.axis_size(axis)
+    blocks = array[None]
+    for level in range(devices.bit_length() - 1):
+        bit = 1 << level
+        other = lax.ppermute(blocks, axis, [(i, i ^ bit) for i in range(devices)])
+        both = jnp.stack([blocks, other])
+        upper = lax.axis_index(axis) >> level & 1
+        blocks = jnp.where(upper == 0, both, both[::-1]).reshape(-1, *array.shape)
+    return blocks
+
+
+def doubled_up(x, axis, dim):
+    return joined_along(collected_by_bits(x, axis), dim)
 
 
 def rotary_tables(capacity, head_dim):
@@ -164,7 +186,7 @@
     shift_two = norm2_shift.astype(jnp.float32)
     qkv_local, qkv_bias_local, out_local = (qkv_weight, qkv_bias, out_weight)
     up_local, up_bias_local, down_local = (up_weight, up_bias, down_weight)
-    row_tokens = lax.all_gather(tokens, "narrow", axis=0, tiled=True)
+    row_tokens = doubled_up(tokens, "narrow", 0)
     slot_count = row_tokens.shape[0]
     projected = jnp.einsum(
         "scd,dje->scje", row_tokens, qkv_local, preferred_element_type=jnp.float32

time: 2790 us -> 2910 us (1.043)
  waiting for transfers between devices: 1790 us -> 1870 us
    ppermute x0 -> x2, waiting for transfers between devices: none -> 251 us  [collected_by_bits(): other = lax.ppermute(blocks, axis, [(i, i ^ bit) for i in range(devices)])]
    all_gather x1 -> x0, waiting for transfers between devices: 167 us -> none  [shards(): row_tokens = lax.all_gather(tokens, 'narrow', axis=0, tiled=True)]
  transfers between devices with their start and end apart: 9 -> 10, of which waited for: 9 -> 10; matrix products, arithmetic and copies ran while one was open for 2% -> 2% of each run, Pallas kernels for 0% -> 0%
where the time goes in v1:
time: 2910 us; the launch traced here: 2900 us
  waiting for transfers between devices  1870 us (64%)
  matrix products  463 us (16%)
  other arithmetic  291 us (10%)
  local copies, waits for them, and re-layouts  158 us (5%)
  loops' own time  49.6 us (2%)
  blocking collectives  42.2 us (1%)
    reduce_scatter x1, waiting for transfers between devices, shards(): lax.psum_scatter(attn_terms, 'narrow', scatter_dimension=0, tiled=True)  314 us
    reduce_scatter x1, waiting for transfers between devices, shards(): lax.psum_scatter(hidden_terms, 'narrow', scatter_dimension=0, tiled=True)  312 us
    reduce_scatter x1, waiting for transfers between devices, shards(): lax.psum_scatter(down_terms, 'narrow', scatter_dimension=0, tiled=True)  311 us
    ppermute x2, waiting for transfers between devices, collected_by_bits(): other = lax.ppermute(blocks, axis, [(i, i ^ bit) for i in range(devices)])  251 us
    all_gather x1, waiting for transfers between devices, shards(): down_grad_rows = lax.all_gather(pre_two_low, 'narrow', axis=0, tiled=True)  168 us
    all_gather x1, waiting for transfers between devices, shards(): out_grad_rows = lax.all_gather(pre_one_low, 'narrow', axis=0, tiled=True)  168 us
    all_gather x1, waiting for transfers between devices, shards(): hidden_rows = lax.all_gather(hidden_low, 'narrow', axis=0, tiled=True)  168 us
    psum x1, waiting for transfers between devices, shards(): lax.psum((qkv_grad, qkv_bias_grad, out_grad, small_grads[4], small_grads[...  114 us
  transfers between devices with their start and end apart: 10, of which 10 were waited for; matrix products, arithmetic and copies ran while one was open for 2% of the time, Pallas kernels for 0%

profile of v1, /device:TPU:0, one launch (start us, length us, event | category | flops | bytes accessed | tf_op | source)
XLA Modules:
  0.0 2897.5 jit_solution(979373673239033721)
XLA Ops:
  10.3 51.5 %collective-permute-done = bf16[1,1,1536,768]{3,2,1,0:T(8,128)(2,1)S(1)} collective-permute-done((bf16[1,1,1536,768]{3,2,1,0:T(8,128)(2,1)}, bf16[1,1,1536,768]{3,2,1,0:T(8,128)(2,1)S(1)}, u32[]{:S(2)}, u32[]{:S(2)}) %collective-permute-start) | collective-permute-done | bytes 2359328 | tf_op jit(solution)/shard_map/ppermute | solution.py:23
  74.5 199.5 %collective-permute-done.1 = bf16[2,1,1536,768]{3,2,0,1:T(8,128)(2,1)} collective-permute-done((bf16[2,1,1536,768]{3,2,0,1:T(8,128)(2,1)}, bf16[2,1,1536,768]{3,2,0,1:T(8,128)(2,1)}, u32[]{:S(2)}, u32[]{:S(2)}) %collective-permute-start.1) | collective-permute-done | bytes 4718624 | tf_op jit(solution)/shard_map/ppermute | solution.py:23
  274.0 8.3 pad_maximum_fusion.1
  282.3 12.2 reverse_select_fusion
  294.6 12.9 broadcast_add_fusion
  320.2 152.3 %while.61 = (s32[]{:T(128)}, bf16[4,1536,3,64]{1,3,2,0:T(8,128)(2,1)}, f32[4,3,3,512]{3,2,1,0:T(4,128)}, bf16[4,1536,3,64]{1,3,2,0:T(8,128)(2,1)}, bf16[4,1536,3...) while((s32[]{:T(128)}, ...), condition=%wide.region_5.6_spmd.clone, body=%wide.region_0.5_spmd.sunk.clone | while | flops 632291328 | bytes 37272460 | solution.py:208
  323.3 30.9 %while.60 = (s32[]{:T(128)}, bf16[3,512,3,64]{1,3,2,0:T(8,128)(2,1)S(1)}, f32[3,3,512]{2,1,0:T(4,128)}, s32[3]{0:T(128)S(1)}, bf16[1536,3,64]{0,2,1:T(8,128)(2,1...) while((s32[]{:T(128)}, ...), condition=%wide.region_4.4_spmd.clone, body=%wide.region_1.3_spmd.clone.sunk | while | flops 632291328 | bytes 30144168 | solution.py:106
  361.3 30.9 %while.60 = (s32[]{:T(128)}, bf16[3,512,3,64]{1,3,2,0:T(8,128)(2,1)S(1)}, f32[3,3,512]{2,1,0:T(4,128)}, s32[3]{0:T(128)S(1)}, bf16[1536,3,64]{0,2,1:T(8,128)(2,1...) while((s32[]{:T(128)}, ...), condition=%wide.region_4.4_spmd.clone, body=%wide.region_1.3_spmd.clone.sunk | while | flops 632291328 | bytes 30144168 | solution.py:106
  399.4 30.9 %while.60 = (s32[]{:T(128)}, bf16[3,512,3,64]{1,3,2,0:T(8,128)(2,1)S(1)}, f32[3,3,512]{2,1,0:T(4,128)}, s32[3]{0:T(128)S(1)}, bf16[1536,3,64]{0,2,1:T(8,128)(2,1...) while((s32[]{:T(128)}, ...), condition=%wide.region_4.4_spmd.clone, body=%wide.region_1.3_spmd.clone.sunk | while | flops 632291328 | bytes 30144168 | solution.py:106
  437.5 30.9 %while.60 = (s32[]{:T(128)}, bf16[3,512,3,64]{1,3,2,0:T(8,128)(2,1)S(1)}, f32[3,3,512]{2,1,0:T(4,128)}, s32[3]{0:T(128)S(1)}, bf16[1536,3,64]{0,2,1:T(8,128)(2,1...) while((s32[]{:T(128)}, ...), condition=%wide.region_4.4_spmd.clone, body=%wide.region_1.3_spmd.clone.sunk | while | flops 632291328 | bytes 30144168 | solution.py:106
  472.5 10.8 fusion.71
  484.1 314.2 %reduce-scatter.5.cloned.1.call-done = f32[1,1536,768]{2,1,0:T(8,128)} async-done(((f32[4,1536,768]{2,1,0:T(8,128)}), f32[1,1536,768]{2,1,0:T(8,128)}) %reduce-scatter.5.cloned.1.call-update) | async-done | bytes 4718608 | tf_op jit(solution)/shard_map/reduce_scatter | solution.py:217
  805.7 167.9 %all-gather.4.cloned.1.call-done = bf16[4,1536,768]{2,1,0:T(8,128)(2,1)} async-done(((bf16[1,1536,768]{2,1,0:T(8,128)(2,1)}), bf16[4,1536,768]{2,1,0:T(8,128)(2,1)}) %all-gather.4.cloned.1.call-update) | async-done | bytes 9437200 | tf_op jit(solution)/shard_map/all_gather | solution.py:223
  973.6 19.4 fusion.55
  993.0 45.9 %multiply_convert_fusion.1 = (bf16[4,1536,768]{2,1,0:T(8,128)(2,1)S(1)}, f32[4,1536,768]{2,1,0:T(8,128)}) fusion(f32[4,1536,768]{2,1,0:T(8,128)} %get-tuple-element.440, f32[768]{0:T(1024)S(1)} %convert_element_type.166, u8[1536,768]{1,0:T(8,128)(4,1)S(1)} %get-tuple-element.302, u8[1536,768]{1,0:T(8,128)(4,1)S(1)} %get-tuple-element.301), kind=kLoop, calls=%fused_computation.65 | loop fusion | flops 335020032 | bytes 49548288 | tf_op jit(solution)/shard_map/convert_element_type | solution.py:227
  1042.6 10.5 fusion.63
  1053.8 311.4 %reduce-scatter.7.cloned.1.call-done = f32[1,1536,768]{2,1,0:T(8,128)} async-done(((f32[4,1536,768]{2,1,0:T(8,128)}), f32[1,1536,768]{2,1,0:T(8,128)}) %reduce-scatter.7.cloned.1.call-update) | async-done | bytes 4718608 | tf_op jit(solution)/shard_map/reduce_scatter | solution.py:229
  1382.2 168.0 %all-gather.6.cloned.1.call-done = bf16[4,1536,768]{2,1,0:T(8,128)(2,1)} async-done(((bf16[1,1536,768]{2,1,0:T(8,128)(2,1)}), bf16[4,1536,768]{2,1,0:T(8,128)(2,1)}) %all-gather.6.cloned.1.call-update) | async-done | bytes 9437200 | tf_op jit(solution)/shard_map/all_gather | solution.py:239
  1550.2 25.1 fusion.83
  1575.3 14.4 fusion.52
  1589.8 312.1 %reduce-scatter.9.cloned.1.call-done = f32[1,1536,768]{2,1,0:T(8,128)} async-done(((f32[4,1536,768]{2,1,0:T(8,128)}), f32[1,1536,768]{2,1,0:T(8,128)}) %reduce-scatter.9.cloned.1.call-update) | async-done | bytes 4718608 | tf_op jit(solution)/shard_map/reduce_scatter | solution.py:254
  1901.9 7.0 multiply_reduce_fusion.1
  1917.2 168.0 %all-gather.8.cloned.1.call-done = bf16[4,1536,768]{2,1,0:T(8,128)(2,1)} async-done(((bf16[1,1536,768]{2,1,0:T(8,128)(2,1)}), bf16[4,1536,768]{2,1,0:T(8,128)(2,1)}) %all-gather.8.cloned.1.call-update) | async-done | bytes 9437200 | tf_op jit(solution)/shard_map/all_gather | solution.py:260
  2085.2 6.9 convolution_convert_fusion
  2097.7 481.3 %while.63 = (s32[]{:T(128)}, f32[4,1536,3,64]{1,3,2,0:T(8,128)}, f32[4,1536,3,64]{1,3,2,0:T(8,128)}, f32[4,1536,3,64]{1,3,2,0:T(8,128)}, f32[4,3,3,512]{3,2,1,0:...) while((s32[]{:T(128)}, f32[4,1536,3,64]{1,3,2,0:T(8,128)}, ...), condition=%wide.region_21.22_spmd.clone, body=%wide.region_17.21_spmd.sunk.clone | while | flops 1532755968 | bytes 175250576 | solution.py:272
  2105.3 104.3 %while.62 = (s32[]{:T(128)}, f32[1536,3,64]{0,2,1:T(8,128)S(1)}, f32[1536,3,64]{0,2,1:T(8,128)S(1)}, f32[3,512,3,64]{1,3,2,0:T(8,128)}, s32[3]{0:T(128)S(1)}, /*...) while((s32[]{:T(128)}, f32[1536,3,64]{0,2,1:T(8,128)S(1)}, ...), condition=%wide.region_20.20_spmd.clone, body=%wide.region_18.19_spmd.clone.sunk | while | flops 1532755968 | bytes 135104288 | solution.py:153
  2113.0 6.6 multiply_reduce_fusion.7
  2119.5 9.4 multiply_convert_fusion.3
  2147.8 6.6 multiply_reduce_fusion.7
  2154.3 9.4 multiply_convert_fusion.3
  2182.6 6.5 multiply_reduce_fusion.7
  2189.1 9.4 multiply_convert_fusion.3
  2225.5 104.3 %while.62 = (s32[]{:T(128)}, f32[1536,3,64]{0,2,1:T(8,128)S(1)}, f32[1536,3,64]{0,2,1:T(8,128)S(1)}, f32[3,512,3,64]{1,3,2,0:T(8,128)}, s32[3]{0:T(128)S(1)}, /*...) while((s32[]{:T(128)}, f32[1536,3,64]{0,2,1:T(8,128)S(1)}, ...), condition=%wide.region_20.20_spmd.clone, body=%wide.region_18.19_spmd.clone.sunk | while | flops 1532755968 | bytes 135104288 | solution.py:153
  2233.2 6.6 multiply_reduce_fusion.7
  2239.8 9.4 multiply_convert_fusion.3
  2268.1 6.6 multiply_reduce_fusion.7
  2274.6 9.4 multiply_convert_fusion.3
  2302.9 6.5 multiply_reduce_fusion.7
  2309.4 9.4 multiply_convert_fusion.3
  2345.8 104.3 %while.62 = (s32[]{:T(128)}, f32[1536,3,64]{0,2,1:T(8,128)S(1)}, f32[1536,3,64]{0,2,1:T(8,128)S(1)}, f32[3,512,3,64]{1,3,2,0:T(8,128)}, s32[3]{0:T(128)S(1)}, /*...) while((s32[]{:T(128)}, f32[1536,3,64]{0,2,1:T(8,128)S(1)}, ...), condition=%wide.region_20.20_spmd.clone, body=%wide.region_18.19_spmd.clone.sunk | while | flops 1532755968 | bytes 135104288 | solution.py:153
  2353.5 6.6 multiply_reduce_fusion.7
  2360.1 9.4 multiply_convert_fusion.3
  2388.3 6.6 multiply_reduce_fusion.7
  2394.9 9.4 multiply_convert_fusion.3
  2423.1 6.5 multiply_reduce_fusion.7
  2429.6 9.4 multiply_convert_fusion.3
  2466.0 104.3 %while.62 = (s32[]{:T(128)}, f32[1536,3,64]{0,2,1:T(8,128)S(1)}, f32[1536,3,64]{0,2,1:T(8,128)S(1)}, f32[3,512,3,64]{1,3,2,0:T(8,128)}, s32[3]{0:T(128)S(1)}, /*...) while((s32[]{:T(128)}, f32[1536,3,64]{0,2,1:T(8,128)S(1)}, ...), condition=%wide.region_20.20_spmd.clone, body=%wide.region_18.19_spmd.clone.sunk | while | flops 1532755968 | bytes 135104288 | solution.py:153
  2473.7 6.6 multiply_reduce_fusion.7
  2480.3 9.4 multiply_convert_fusion.3
  2508.6 6.6 multiply_reduce_fusion.7
  2515.1 9.4 multiply_convert_fusion.3
  2543.4 6.5 multiply_reduce_fusion.7
  2549.9 9.4 multiply_convert_fusion.3
  2579.0 6.5 multiply_subtract_fusion.1
  2592.1 10.1 bitcast_convert_fusion
  2602.4 15.2 convolution_bitcast_fusion
  2617.5 14.2 fusion.59
  2631.8 6.5 convolution_bitcast_fusion.2
  2638.4 11.1 convolution_bitcast_fusion.1
  2650.2 17.9 all-reduce.2
  2668.1 5.7 fusion.41
  2673.9 24.3 all-reduce
  2698.2 64.8 %reduce-scatter.11.cloned.1.call-done = bf16[1,1536,768]{2,1,0:T(8,128)(2,1)} async-done(((bf16[4,1536,768]{2,1,0:T(8,128)(2,1)}), bf16[1,1536,768]{2,1,0:T(8,128)(2,1)}) %reduce-scatter.11.cloned.1.call-update) | async-done | bytes 2359312 | tf_op jit(solution)/shard_map/reduce_scatter | solution.py:288
  2768.7 113.9 %all-reduce.5.cloned.1.call-done = (f32[768,3,192]{0,2,1:T(8,128)}, f32[192,768]{1,0:T(8,128)}, f32[768,768]{1,0:T(8,128)}, f32[768,768]{1,0:T(8,128)}) async-done(((f32[768,3,192]{0,2,1:T(8,128)}, f32[192,768]{1,0:T(8,128)}, f32[768,768]{1,0:T(8,128)}, f32[768,768]{1,0:T(8,128)}), (f32[768,3,192]{0,2,1:T(8,128)}, f32[192,768]{1,0:T(8,128)}, f32[768,768]{1,0:T(8,128)}, ...) | async-done | bytes 7077904 | tf_op jit(solution)/shard_map/psum | solution.py:303
  (481 shorter events, 485.7 us)
Async XLA Ops:
  7.2 966.4 %copy-start = (bf16[768,768]{1,0:T(8,128)(2,1)S(1)}, bf16[768,768]{1,0:T(8,128)(2,1)}, u32[]{:S(2)}) copy-start(bf16[768,768]{1,0:T(8,128)(2,1)} %param.31) | copy-start | bytes 3538948
  7.2 791.1 %reduce-scatter.5.cloned.1.call-start = ((), (), s32[]{:S(2)}) async-start(), calls=%async_computation.4 | async-start | bytes 23592960 | tf_op jit(solution)/shard_map/reduce_scatter | solution.py:217
  7.2 54.5 %collective-permute-start = (bf16[1,1,1536,768]{3,2,1,0:T(8,128)(2,1)}, bf16[1,1,1536,768]{3,2,1,0:T(8,128)(2,1)S(1)}, u32[]{:S(2)}, u32[]{:S(2)}) collective-permute-start(bf16[1,1,1536,768]{3,2,1,0:T(8,128)(2,1)} %bitcast.231), channel_id=1, source_target_pairs={{0,1},{1,0},{2,3},{3,2},{4,5},{5,4},{6,7},{7,6},{8,9},{9,8},{10,11... | collective-permute-start | bytes 7077896 | tf_op jit(solution)/shard_map/ppermute | solution.py:23
  63.9 7.5 copy-start.28
  68.7 205.3 %collective-permute-start.1 = (bf16[2,1,1536,768]{3,2,0,1:T(8,128)(2,1)}, bf16[2,1,1536,768]{3,2,0,1:T(8,128)(2,1)}, u32[]{:S(2)}, u32[]{:S(2)}) collective-permute-start(bf16[2,1,1536,768]{3,2,0,1:T(8,128)(2,1)} %get-tuple-element.432), channel_id=1, source_target_pairs={{0,2},{1,3},{2,0},{3,1},{4,6},{5,7},{6,4},{7,5},{8,10},{9,11},{10,... | collective-permute-start | bytes 14155784 | tf_op jit(solution)/shard_map/ppermute | solution.py:23
  74.5 241.7 %copy-start.19 = (f32[1536,32]{0,1:T(8,128)}, f32[1536,32]{0,1:T(8,128)S(1)}, u32[]{:S(2)}) copy-start(f32[1536,32]{0,1:T(8,128)S(1)} %get-tuple-element.439) | copy-start | bytes 589828
  282.3 12.2 copy-start.37
  483.3 315.0 %copy-start.14 = (bf16[1,1536,768]{2,1,0:T(8,128)(2,1)S(1)}, bf16[1,1536,768]{2,1,0:T(8,128)(2,1)}, u32[]{:S(2)}) copy-start(bf16[1,1536,768]{2,1,0:T(8,128)(2,1)} %param.23) | copy-start | bytes 7077892
  483.4 490.2 %all-gather.4.cloned.1.call-start = ((), (), s32[]{:S(2)}) async-start(), calls=%async_computation.5 | async-start | bytes 11796480 | tf_op jit(solution)/shard_map/all_gather | solution.py:223
  805.6 559.6 %reduce-scatter.7.cloned.1.call-start = ((), (), s32[]{:S(2)}) async-start(), calls=%async_computation.6 | async-start | bytes 23592960 | tf_op jit(solution)/shard_map/reduce_scatter | solution.py:229
  993.0 49.6 %copy-start.36 = (bf16[768,768]{1,0:T(8,128)(2,1)S(1)}, bf16[768,768]{1,0:T(8,128)(2,1)}, u32[]{:S(2)}) copy-start(bf16[768,768]{1,0:T(8,128)(2,1)} %param.33) | copy-start | bytes 3538948
  1053.1 497.0 %all-gather.6.cloned.1.call-start = ((), (), s32[]{:S(2)}) async-start(), calls=%async_computation.7 | async-start | bytes 11796480 | tf_op jit(solution)/shard_map/all_gather | solution.py:239
  1382.2 519.7 %reduce-scatter.9.cloned.1.call-start = ((), (), s32[]{:S(2)}) async-start(), calls=%async_computation.8 | async-start | bytes 23592960 | tf_op jit(solution)/shard_map/reduce_scatter | solution.py:254
  1589.7 495.4 %all-gather.8.cloned.1.call-start = ((), (), s32[]{:S(2)}) async-start(), calls=%async_computation.9 | async-start | bytes 11796480 | tf_op jit(solution)/shard_map/all_gather | solution.py:260
  1915.5 169.7 %copy-start.20 = (bf16[192,768]{1,0:T(8,128)(2,1)S(1)}, bf16[192,768]{1,0:T(8,128)(2,1)}, u32[]{:S(2)}) copy-start(bf16[192,768]{1,0:T(8,128)(2,1)} %param.27) | copy-start | bytes 884740
  1917.2 845.8 %reduce-scatter.11.cloned.1.call-start = ((), (), s32[]{:S(2)}) async-start(), calls=%async_computation.10 | async-start | bytes 11796480 | tf_op jit(solution)/shard_map/reduce_scatter | solution.py:288
  2092.1 5.6 copy-start.40
  2097.9 7.4 copy-start.15
  2113.0 6.6 copy-start.2
  2128.9 3.9 copy-start.3
  2147.8 6.6 copy-start.2
  2163.7 3.9 copy-start.3
  2182.6 6.5 copy-start.2
  2198.5 3.8 copy-start.3
  2211.3 6.9 copy-start.16
  2218.2 7.4 copy-start.15
  2233.2 6.6 copy-start.2
  2249.2 3.9 copy-start.3
  2268.1 6.6 copy-start.2
  2284.0 3.9 copy-start.3
  2302.9 6.5 copy-start.2
  2318.8 3.8 copy-start.3
  2331.6 6.8 copy-start.16
  2338.4 7.4 copy-start.15
  2353.5 6.6 copy-start.2
  2369.4 3.9 copy-start.3
  2388.3 6.6 copy-start.2
  2404.3 3.9 copy-start.3
  2423.1 6.5 copy-start.2
  2439.0 3.8 copy-start.3
  2451.8 6.8 copy-start.16
  2458.7 7.4 copy-start.15
  2473.7 6.6 copy-start.2
  2489.7 3.9 copy-start.3
  2508.6 6.6 copy-start.2
  2524.5 3.9 copy-start.3
  2543.4 6.5 copy-start.2
  2559.3 3.8 copy-start.3
  2572.1 6.9 copy-start.16
  2585.5 6.3 slice-start.4
  2588.0 3.8 slice-start.5
  2588.0 4.1 copy-start.38
  2602.3 280.3 %all-reduce.5.cloned.1.call-start = ((), (), s32[]{:S(2)}) async-start(), calls=%async_computation.11 | async-start | bytes 14155776 | tf_op jit(solution)/shard_map/psum | solution.py:303
  2602.3 36.0 %slice-start = ((s8[4718592]{0:T(1024)(128)(4,1)}), s8[4194304]{0:T(1024)(128)(4,1)S(1)}, s32[]{:S(2)}) async-start(s8[4718592]{0:T(1024)(128)(4,1)} %bitcast.212), calls=%async_computation.12 | async-start | bytes 8388608
  2602.4 36.0 %slice-start.2 = ((s8[4718592]{0:T(1024)(128)(4,1)}), s8[4194304]{0:T(1024)(128)(4,1)S(1)}, s32[]{:S(2)}) async-start(s8[4718592]{0:T(1024)(128)(4,1)} %bitcast.217), calls=%async_computation.14 | async-start | bytes 8388608
  2602.4 35.9 %slice-start.6 = ((s8[4718592]{0:T(1024)(128)(4,1)}), s8[4194304]{0:T(1024)(128)(4,1)S(1)}, s32[]{:S(2)}) async-start(s8[4718592]{0:T(1024)(128)(4,1)} %bitcast.224), calls=%async_computation.18 | async-start | bytes 8388608
  2617.5 14.3 copy-start.13
  2617.5 20.8 slice-start.1
  2617.5 20.8 slice-start.3
  2617.5 20.8 slice-start.7
  2668.1 5.8 copy-start.27
  2882.6 5.0 copy-start.18
  2882.6 6.4 copy-start.17
  2885.6 4.8 copy-start.1
  (26 other events, 39.4 us)
Sparse Core Ops, SparseCore 0:
  483.5 314.7 reduce-scatter.4
  805.7 167.8 all-gather.3
  1053.3 311.9 reduce-scatter.6
  1382.3 167.8 all-gather.5
  1589.9 311.9 reduce-scatter.8
  1917.3 167.8 all-gather.7
  2602.4 160.5 reduce-scatter.10
  2768.3 114.3 all-reduce.4
